TPU v7x, 32 devices: a whole 2x2x4 slice. The times are simulated.
32 devices in a mesh: pair: 8 (over z, x), col: 4 (over y, core).
Axes of the slice: x: 2, y: 2, z: 4, core: 2. Of those that a mesh axis runs over, the one named last changes fastest.
Arguments:
- point_values: bfloat16 [32768, 1024], P('pair', 'col'), may hold values from -2 to 2, as said below
- grid_values: bfloat16 [32768, 512], P('pair'), may hold values from -6 to 6
Outputs:
- fitted: float32 [512, 1024], P(('pair', 'col'))
Inputs may be any that keep to these rules, and one draw needn't show every extreme that they name: `point_values`: real pair-product values.
All inputs are finite; a program needn't handle non-finite values.
Results may differ from a plain program's by a relative error of at most 0.0003.
Values may be sent and summed in bfloat16 or wider, within the bound.
A program may use at most 128 MiB of HBM per device.

v0:
```python
import jax
import jax.numpy as jnp
from jax import lax
from jax.sharding import PartitionSpec as P


def cross(left, right):
    return lax.dot_general(
        left, right, (((0,), (0,)), ((), ())), preferred_element_type=jnp.float32
    )


def body(point_values, grid_values):
    gathered = lax.all_gather(point_values, "col", axis=1, tiled=True)
    gram = lax.psum(cross(gathered, gathered), "pair")
    factor = jnp.linalg.cholesky(gram)
    summed = lax.psum_scatter(
        cross(grid_values, point_values), "pair", scatter_dimension=0, tiled=True
    )
    regrouped = lax.all_to_all(summed, "col", split_axis=0, concat_axis=1, tiled=True)
    solved = jax.scipy.linalg.cho_solve((factor, True), regrouped.T)
    return solved.T


def solution(mesh):
    in_specs = (P("pair", "col"), P("pair", None))
    out_specs = P(("pair", "col"), None)
    return jax.shard_map(body, mesh=mesh, in_specs=in_specs, out_specs=out_specs, check_vma=False)
```

profile of v0, /device:TPU:0, one launch (start us, length us, event | category | flops | bytes accessed | tf_op | source)
XLA Modules:
  0.0 594.1 jit_solution(14145770324071007327)
XLA Ops:
  8.1 5.0 fusion.96
  13.2 58.8 %all-gather.2.cloned.1.call-done = bf16[4096,1024]{1,0:T(8,128)(2,1)} async-done(((bf16[4096,256]{1,0:T(8,128)(2,1)}), bf16[4096,1024]{1,0:T(8,128)(2,1)}) %all-gather.2.cloned.1.call-update) | async-done | bytes 8388624 | tf_op jit(solution)/shard_map/all_gather | solution.py:14
  72.0 15.1 %fusion.95 = f32[1024,1024]{0,1:T(8,128)} fusion(bf16[4096,1024]{1,0:T(8,128)(2,1)} %all-gather.2.cloned.1.call-done), kind=kOutput, calls=%fused_computation.213 | convolution fusion | flops 8589934592 | bytes 12582912 | tf_op jit(solution)/shard_map/dot_general | solution.py:8
  87.1 3.3 all-to-all-start
  90.4 4.1 all-to-all-done
  94.5 148.8 %all-reduce.3.cloned.1.call-done = f32[1024,1024]{0,1:T(8,128)} async-done(((f32[1024,1024]{0,1:T(8,128)}), f32[1024,1024]{0,1:T(8,128)}) %all-reduce.3.cloned.1.call-update) | async-done | bytes 4194320 | tf_op jit(solution)/shard_map/psum | solution.py:15
  243.3 5.6 copy.9
  248.9 4.4 fusion
  253.4 1.9 copy-done
  255.3 11.7 %cholesky.223 = f32[128,128]{1,0:T(8,128)S(1)} custom-call(f32[128,128]{1,0:T(8,128)S(1)} %cholesky.580), custom_call_target="Cholesky" | custom-call | tf_op jit(solution)/shard_map/jit(cholesky)/cholesky | solution.py:16
  267.0 9.8 %custom-call.66 = f32[1,128,128]{1,2,0:T(8,128)S(1)} custom-call(f32[1,128,128]{2,1,0:T(8,128)S(1)} %get-tuple-element.44), custom_call_target="InvertDiagBlocksLowerTriangular" | custom-call | tf_op jit(solution)/shard_map/jit(cholesky)/cholesky | solution.py:16
  276.9 2.5 cholesky.255
  279.4 2.4 constant_dynamic-update-slice_fusion.50
  281.7 1.5 convolution_subtract_fusion
  283.3 12.2 %cholesky.244 = f32[128,128]{1,0:T(8,128)S(1)} custom-call(f32[128,128]{1,0:T(8,128)S(1)} %cholesky.584), custom_call_target="Cholesky" | custom-call | tf_op jit(solution)/shard_map/jit(cholesky)/cholesky | solution.py:16
  296.2 9.8 %custom-call.67 = f32[1,128,128]{1,2,0:T(8,128)S(1)} custom-call(f32[1,128,128]{2,1,0:T(8,128)S(1)} %get-tuple-element.41), custom_call_target="InvertDiagBlocksLowerTriangular" | custom-call | tf_op jit(solution)/shard_map/jit(cholesky)/cholesky | solution.py:16
  306.0 1.2 convolution_dynamic-update-slice_fusion
  307.2 2.1 convolution_subtract_fusion.1
  309.3 11.7 %cholesky.468 = f32[128,128]{1,0:T(8,128)S(1)} custom-call(f32[128,128]{1,0:T(8,128)S(1)} %cholesky.589), custom_call_target="Cholesky" | custom-call | tf_op jit(solution)/shard_map/jit(cholesky)/cholesky | solution.py:16
  322.3 9.8 %custom-call.68 = f32[1,128,128]{1,2,0:T(8,128)S(1)} custom-call(f32[1,128,128]{2,1,0:T(8,128)S(1)} %get-tuple-element.38), custom_call_target="InvertDiagBlocksLowerTriangular" | custom-call | tf_op jit(solution)/shard_map/jit(cholesky)/cholesky | solution.py:16
  332.1 1.2 convolution_dynamic-update-slice_fusion.1
  333.3 2.3 convolution_subtract_fusion.2
  335.6 11.8 %cholesky.487 = f32[128,128]{1,0:T(8,128)S(1)} custom-call(f32[128,128]{1,0:T(8,128)S(1)} %cholesky.594), custom_call_target="Cholesky" | custom-call | tf_op jit(solution)/shard_map/jit(cholesky)/cholesky | solution.py:16
  348.8 9.8 %custom-call.69 = f32[1,128,128]{1,2,0:T(8,128)S(1)} custom-call(f32[1,128,128]{2,1,0:T(8,128)S(1)} %get-tuple-element.35), custom_call_target="InvertDiagBlocksLowerTriangular" | custom-call | tf_op jit(solution)/shard_map/jit(cholesky)/cholesky | solution.py:16
  358.6 1.1 convolution_dynamic-update-slice_fusion.2
  359.7 2.3 convolution_subtract_fusion.3
  362.0 11.7 %cholesky.506 = f32[128,128]{1,0:T(8,128)S(1)} custom-call(f32[128,128]{1,0:T(8,128)S(1)} %cholesky.599), custom_call_target="Cholesky" | custom-call | tf_op jit(solution)/shard_map/jit(cholesky)/cholesky | solution.py:16
  375.0 10.0 %custom-call.70 = f32[1,128,128]{1,2,0:T(8,128)S(1)} custom-call(f32[1,128,128]{2,1,0:T(8,128)S(1)} %get-tuple-element.32), custom_call_target="InvertDiagBlocksLowerTriangular" | custom-call | tf_op jit(solution)/shard_map/jit(cholesky)/cholesky | solution.py:16
  385.0 1.0 convolution_dynamic-update-slice_fusion.3
  386.0 2.3 convolution_subtract_fusion.4
  388.3 11.7 %cholesky.526 = f32[128,128]{1,0:T(8,128)S(1)} custom-call(f32[128,128]{1,0:T(8,128)S(1)} %cholesky.604), custom_call_target="Cholesky" | custom-call | tf_op jit(solution)/shard_map/jit(cholesky)/cholesky | solution.py:16
  401.3 9.8 %custom-call.71 = f32[1,128,128]{1,2,0:T(8,128)S(1)} custom-call(f32[1,128,128]{2,1,0:T(8,128)S(1)} %get-tuple-element.29), custom_call_target="InvertDiagBlocksLowerTriangular" | custom-call | tf_op jit(solution)/shard_map/jit(cholesky)/cholesky | solution.py:16
  411.1 0.9 convolution_dynamic-update-slice_fusion.4
  412.1 2.0 convolution_subtract_fusion.5
  414.1 12.1 %cholesky.546 = f32[128,128]{1,0:T(8,128)S(1)} custom-call(f32[128,128]{1,0:T(8,128)S(1)} %cholesky.609), custom_call_target="Cholesky" | custom-call | tf_op jit(solution)/shard_map/jit(cholesky)/cholesky | solution.py:16
  427.5 9.8 %custom-call.72 = f32[1,128,128]{1,2,0:T(8,128)S(1)} custom-call(f32[1,128,128]{2,1,0:T(8,128)S(1)} %get-tuple-element.26), custom_call_target="InvertDiagBlocksLowerTriangular" | custom-call | tf_op jit(solution)/shard_map/jit(cholesky)/cholesky | solution.py:16
  437.3 0.8 convolution_dynamic-update-slice_fusion.5
  438.1 1.8 convolution_subtract_fusion.6
  439.9 11.7 %cholesky.564 = f32[128,128]{1,0:T(8,128)S(1)} custom-call(f32[128,128]{1,0:T(8,128)S(1)} %convolution_subtract_fusion.6), custom_call_target="Cholesky" | custom-call | tf_op jit(solution)/shard_map/jit(cholesky)/cholesky | solution.py:16
  458.5 4.8 select_select_fusion
  463.2 22.8 %while.1 = (s32[]{:T(128)}, f32[1024,1024]{1,0:T(8,128)}, s32[8,2]{0,1:T(2,128)S(1)}, f32[8,128,128]{2,1,0:T(8,128)S(1)}, s32[]{:T(128)}) while((s32[]{:T(128)}, f32[1024,1024]{1,0:T(8,128)}, s32[8,2]{0,1:T(2,128)S(1)}, f32[8,128,128]{2,1,0:T(8,128)S(1)}, s32[]{:T(128)}) %tuple.56), condition=%wide.while_cond, body=%wide.while_body.sunk | while | flops 2 | bytes 131181 | solution.py:21
  463.9 2.2 bitcast_dynamic-update-slice_fusion.2
  466.7 2.2 bitcast_dynamic-update-slice_fusion.2
  469.6 2.2 bitcast_dynamic-update-slice_fusion.2
  472.5 2.2 bitcast_dynamic-update-slice_fusion.2
  475.3 2.2 bitcast_dynamic-update-slice_fusion.2
  478.2 2.2 bitcast_dynamic-update-slice_fusion.2
  481.1 2.2 bitcast_dynamic-update-slice_fusion.2
  483.9 2.2 bitcast_dynamic-update-slice_fusion.2
  486.1 78.8 %custom-call.73 = f32[8,128,128]{1,2,0:T(8,128)S(1)} custom-call(f32[8,128,128]{2,1,0:T(8,128)S(1)} %get-tuple-element.12), custom_call_target="InvertDiagBlocksLowerTriangular" | custom-call | tf_op jit(solution)/shard_map/jit(_cho_solve)/triangular_solve | solution.py:21
  565.0 1.0 convolution_subtract_fusion.14
  566.3 1.1 convolution_subtract_fusion.13
  567.6 1.3 convolution_subtract_fusion.12
  569.0 1.2 convolution_subtract_fusion.11
  570.4 1.4 convolution_subtract_fusion.20
  572.0 1.4 convolution_subtract_fusion.19
  573.6 1.6 convolution_subtract_fusion.18
  575.5 1.0 convolution_subtract_fusion.10
  576.8 1.1 convolution_subtract_fusion.9
  578.1 1.2 convolution_subtract_fusion.8
  579.5 1.2 convolution_subtract_fusion.7
  581.0 1.3 convolution_subtract_fusion.17
  582.6 1.3 convolution_subtract_fusion.16
  584.2 1.4 convolution_subtract_fusion.15
  (90 shorter events, 18.8 us)
Async XLA Ops:
  7.4 64.6 %all-gather.2.cloned.1.call-start = ((), (), s32[]{:S(2)}) async-start(), calls=%async_computation.2 | async-start | bytes 10485760 | tf_op jit(solution)/shard_map/all_gather | solution.py:14
  8.1 79.0 %reduce-scatter.2.cloned.1.call-start = ((), (), s32[]{:S(2)}) async-start(), calls=%async_computation.4 | async-start | bytes 589824 | tf_op jit(solution)/shard_map/reduce_scatter | solution.py:17
  13.1 230.2 %all-reduce.3.cloned.1.call-start = ((), (), s32[]{:S(2)}) async-start(), calls=%async_computation.3 | async-start | bytes 8388608 | tf_op jit(solution)/shard_map/psum | solution.py:15
  87.1 7.4 %all-to-all-start = ((f32[4,16,256]{2,1,0:T(8,128)}), f32[4,16,256]{2,1,0:T(8,128)S(1)}, u32[]{:S(2)}, u32[]{:S(2)}) async-start(f32[4,16,256]{2,1,0:T(8,128)} %bitcast.147), calls=%async_computation.1 | async-start | bytes 131072 | tf_op jit(solution)/shard_map/all_to_all | solution.py:20
  253.4 1.9 copy-start
  585.8 0.6 copy-start.1
Sparse Core Ops, SparseCore 0:
  9.8 62.1 all-gather.1
Sparse Core Ops, SparseCore 1:
  13.2 64.7 reduce-scatter.1
  87.2 156.1 all-reduce.2
where the time goes:
time: 600 us; the launch traced here: 594 us
  other arithmetic  261 us (44%)
  waiting for transfers between devices  212 us (35%)
  matrix products  63.6 us (11%)
  local copies, waits for them, and re-layouts  33.6 us (6%)
  between operations  20.3 us (3%)
    another operation x30, other arithmetic, body(): factor = jnp.linalg.cholesky(gram)  173 us
    psum x1, waiting for transfers between devices, body(): gram = lax.psum(cross(gathered, gathered), 'pair')  149 us
    another operation x3, other arithmetic, body(): solved = jax.scipy.linalg.cho_solve((factor, True), regrouped.T)  83.6 us
    all_gather x1, waiting for transfers between devices, body(): gathered = lax.all_gather(point_values, 'col', axis=1, tiled=True)  58.8 us
    another operation x14, matrix products, body(): factor = jnp.linalg.cholesky(gram)  23.1 us
    another operation x24, local copies, waits for them, and re-layouts  22.7 us
    another operation x30, matrix products, body(): solved = jax.scipy.linalg.cho_solve((factor, True), regrouped.T)  20.5 us
    dot_general x2, matrix products, cross(): lax.dot_general(left, right, (((0,), (0,)), ((), ())), preferred_element_...  20 us
  transfers between devices with their start and end apart: 4, of which 3 were waited for; matrix products, arithmetic and copies ran while one was open for 3% of the time, Pallas kernels for 0%

commit v1 on v0

--- a/solution.py
+++ b/solution.py
@@ -12,7 +12,8 @@
 
 def body(point_values, grid_values):
     gathered = lax.all_gather(point_values, "col", axis=1, tiled=True)
-    gram = lax.psum(cross(gathered, gathered), "pair")
+    u_in = cross(gathered, gathered)
+    gram = jnp.sum(lax.all_gather(u_in, "pair"), axis=0)
     factor = jnp.linalg.cholesky(gram)
     summed = lax.psum_scatter(
         cross(grid_values, point_values), "pair", scatter_dimension=0, tiled=True

time: 600 us -> 1100 us (1.83)
  waiting for transfers between devices: 212 us -> 694 us
  other arithmetic: 261 us -> 275 us
    all_gather x0 -> x1, waiting for transfers between devices: none -> 630 us  [body(): gram = jnp.sum(lax.all_gather(u_in, 'pair'), axis=0)]
    psum x1 -> x0, waiting for transfers between devices: 149 us -> none  [body(): gram = lax.psum(cross(gathered, gathered), 'pair')]
    reduce_sum x0 -> x1, other arithmetic: none -> 14.7 us  [body(): gram = jnp.sum(lax.all_gather(u_in, 'pair'), axis=0)]
  transfers between devices with their start and end apart: 4 -> 4, of which waited for: 3 -> 3; matrix products, arithmetic and copies ran while one was open for 3% -> 2% of each run, Pallas kernels for 0% -> 0%
where the time goes in v1:
time: 1100 us; the launch traced here: 1090 us
  waiting for transfers between devices  694 us (63%)
  other arithmetic  275 us (25%)
  matrix products  63.7 us (6%)
  local copies, waits for them, and re-layouts  33.6 us (3%)
  between operations  20.3 us (2%)
    all_gather x1, waiting for transfers between devices, body(): gram = jnp.sum(lax.all_gather(u_in, 'pair'), axis=0)  630 us
    another operation x30, other arithmetic, body(): factor = jnp.linalg.cholesky(gram)  173 us
    another operation x3, other arithmetic, body(): solved = jax.scipy.linalg.cho_solve((factor, True), regrouped.T)  83.6 us
    all_gather x1, waiting for transfers between devices, body(): gathered = lax.all_gather(point_values, 'col', axis=1, tiled=True)  58.8 us
    another operation x14, matrix products, body(): factor = jnp.linalg.cholesky(gram)  23.1 us
    another operation x24, local copies, waits for them, and re-layouts  22.7 us
  transfers between devices with their start and end apart: 4, of which 3 were waited for; matrix products, arithmetic and copies ran while one was open for 2% of the time, Pallas kernels for 0%

profile of v1, /device:TPU:0, one launch (start us, length us, event | category | flops | bytes accessed | tf_op | source)
XLA Modules:
  0.0 1090.5 jit_solution(5713015690415199770)
XLA Ops:
  8.1 5.0 fusion.96
  13.2 58.8 %all-gather.4.cloned.1.call-done = bf16[4096,1024]{1,0:T(8,128)(2,1)} async-done(((bf16[4096,256]{1,0:T(8,128)(2,1)}), bf16[4096,1024]{1,0:T(8,128)(2,1)}) %all-gather.4.cloned.1.call-update) | async-done | bytes 8388624 | tf_op jit(solution)/shard_map/all_gather | solution.py:14
  72.0 15.2 %fusion.95 = f32[1024,1024]{1,0:T(8,128)} fusion(bf16[4096,1024]{1,0:T(8,128)(2,1)} %all-gather.4.cloned.1.call-done), kind=kOutput, calls=%fused_computation.213 | convolution fusion | flops 8589934592 | bytes 12582912 | tf_op jit(solution)/shard_map/dot_general | solution.py:8
  87.2 3.3 all-to-all-start
  90.5 4.1 all-to-all-done
  94.6 630.4 %all-gather.6.cloned.1.call-done = f32[8192,1024]{1,0:T(8,128)} async-done(((f32[1024,1024]{1,0:T(8,128)}), f32[8192,1024]{1,0:T(8,128)}) %all-gather.6.cloned.1.call-update) | async-done | bytes 33554448 | tf_op jit(solution)/shard_map/all_gather | solution.py:16
  725.0 14.7 %reduce_sum.9 = f32[1024,1024]{1,0:T(8,128)} reduce(f32[8,1024,1024]{2,1,0:T(8,128)} %bitcast.139, f32[]{:T(128)} %constant.276.clone.1), dimensions={0}, to_apply=%region_0.0 | reduce | flops 7340032 | bytes 37748740 | tf_op jit(solution)/shard_map/reduce_sum | solution.py:16
  739.7 5.6 copy.6
  745.3 4.4 fusion
  749.8 1.9 copy-done
  751.7 11.7 %cholesky.223 = f32[128,128]{1,0:T(8,128)S(1)} custom-call(f32[128,128]{1,0:T(8,128)S(1)} %cholesky.580), custom_call_target="Cholesky" | custom-call | tf_op jit(solution)/shard_map/jit(cholesky)/cholesky | solution.py:17
  763.4 2.5 cholesky.255
  765.9 9.8 custom-call.66
  775.7 2.4 constant_dynamic-update-slice_fusion.50
  778.1 1.5 convolution_subtract_fusion
  779.7 12.2 %cholesky.244 = f32[128,128]{1,0:T(8,128)S(1)} custom-call(f32[128,128]{1,0:T(8,128)S(1)} %cholesky.584), custom_call_target="Cholesky" | custom-call | tf_op jit(solution)/shard_map/jit(cholesky)/cholesky | solution.py:17
  792.5 9.8 custom-call.67
  802.4 1.2 convolution_dynamic-update-slice_fusion
  803.6 2.1 convolution_subtract_fusion.1
  805.7 11.7 %cholesky.468 = f32[128,128]{1,0:T(8,128)S(1)} custom-call(f32[128,128]{1,0:T(8,128)S(1)} %cholesky.589), custom_call_target="Cholesky" | custom-call | tf_op jit(solution)/shard_map/jit(cholesky)/cholesky | solution.py:17
  818.7 9.8 custom-call.68
  828.5 1.2 convolution_dynamic-update-slice_fusion.1
  829.7 2.3 convolution_subtract_fusion.2
  832.0 11.8 %cholesky.487 = f32[128,128]{1,0:T(8,128)S(1)} custom-call(f32[128,128]{1,0:T(8,128)S(1)} %cholesky.594), custom_call_target="Cholesky" | custom-call | tf_op jit(solution)/shard_map/jit(cholesky)/cholesky | solution.py:17
  845.2 9.8 custom-call.69
  855.0 1.1 convolution_dynamic-update-slice_fusion.2
  856.1 2.3 convolution_subtract_fusion.3
  858.4 11.7 %cholesky.506 = f32[128,128]{1,0:T(8,128)S(1)} custom-call(f32[128,128]{1,0:T(8,128)S(1)} %cholesky.599), custom_call_target="Cholesky" | custom-call | tf_op jit(solution)/shard_map/jit(cholesky)/cholesky | solution.py:17
  871.4 10.0 custom-call.70
  881.4 1.0 convolution_dynamic-update-slice_fusion.3
  882.4 2.3 convolution_subtract_fusion.4
  884.7 11.7 %cholesky.526 = f32[128,128]{1,0:T(8,128)S(1)} custom-call(f32[128,128]{1,0:T(8,128)S(1)} %cholesky.604), custom_call_target="Cholesky" | custom-call | tf_op jit(solution)/shard_map/jit(cholesky)/cholesky | solution.py:17
  897.7 9.8 custom-call.71
  907.5 0.9 convolution_dynamic-update-slice_fusion.4
  908.5 2.0 convolution_subtract_fusion.5
  910.5 12.1 %cholesky.546 = f32[128,128]{1,0:T(8,128)S(1)} custom-call(f32[128,128]{1,0:T(8,128)S(1)} %cholesky.609), custom_call_target="Cholesky" | custom-call | tf_op jit(solution)/shard_map/jit(cholesky)/cholesky | solution.py:17
  923.9 9.8 custom-call.72
  934.5 1.8 convolution_subtract_fusion.6
  936.3 11.7 %cholesky.564 = f32[128,128]{1,0:T(8,128)S(1)} custom-call(f32[128,128]{1,0:T(8,128)S(1)} %convolution_subtract_fusion.6), custom_call_target="Cholesky" | custom-call | tf_op jit(solution)/shard_map/jit(cholesky)/cholesky | solution.py:17
  954.8 4.8 select_select_fusion
  959.6 22.8 %while.1 = (s32[]{:T(128)}, f32[1024,1024]{1,0:T(8,128)}, s32[8,2]{0,1:T(2,128)S(1)}, f32[8,128,128]{2,1,0:T(8,128)S(1)}, s32[]{:T(128)}) while((s32[]{:T(128)}, f32[1024,1024]{1,0:T(8,128)}, s32[8,2]{0,1:T(2,128)S(1)}, f32[8,128,128]{2,1,0:T(8,128)S(1)}, s32[]{:T(128)}) %tuple.56), condition=%wide.while_cond, body=%wide.while_body.sunk | while | flops 2 | bytes 131181 | solution.py:22
  960.3 2.2 bitcast_dynamic-update-slice_fusion.2
  963.1 2.2 bitcast_dynamic-update-slice_fusion.2
  966.0 2.2 bitcast_dynamic-update-slice_fusion.2
  968.9 2.2 bitcast_dynamic-update-slice_fusion.2
  971.7 2.2 bitcast_dynamic-update-slice_fusion.2
  974.6 2.2 bitcast_dynamic-update-slice_fusion.2
  977.5 2.2 bitcast_dynamic-update-slice_fusion.2
  980.3 2.2 bitcast_dynamic-update-slice_fusion.2
  982.5 78.8 %custom-call.73 = f32[8,128,128]{1,2,0:T(8,128)S(1)} custom-call(f32[8,128,128]{2,1,0:T(8,128)S(1)} %get-tuple-element.12), custom_call_target="InvertDiagBlocksLowerTriangular" | custom-call | tf_op jit(solution)/shard_map/jit(_cho_solve)/triangular_solve | solution.py:22
  1061.4 1.0 convolution_subtract_fusion.14
  1062.7 1.1 convolution_subtract_fusion.13
  1064.0 1.3 convolution_subtract_fusion.12
  1065.4 1.2 convolution_subtract_fusion.11
  1066.8 1.4 convolution_subtract_fusion.20
  1068.4 1.4 convolution_subtract_fusion.19
  1070.0 1.6 convolution_subtract_fusion.18
  1071.9 1.0 convolution_subtract_fusion.10
  1073.2 1.1 convolution_subtract_fusion.9
  1074.5 1.2 convolution_subtract_fusion.8
  1075.9 1.2 convolution_subtract_fusion.7
  1077.4 1.3 convolution_subtract_fusion.17
  1079.0 1.3 convolution_subtract_fusion.16
  1080.6 1.4 convolution_subtract_fusion.15
  (91 shorter events, 19.6 us)
Async XLA Ops:
  7.4 64.6 %all-gather.4.cloned.1.call-start = ((), (), s32[]{:S(2)}) async-start(), calls=%async_computation.2 | async-start | bytes 10485760 | tf_op jit(solution)/shard_map/all_gather | solution.py:14
  8.1 79.1 %reduce-scatter.2.cloned.1.call-start = ((), (), s32[]{:S(2)}) async-start(), calls=%async_computation.3 | async-start | bytes 589824 | tf_op jit(solution)/shard_map/reduce_scatter | solution.py:18
  13.1 711.9 %all-gather.6.cloned.1.call-start = ((), (), s32[]{:S(2)}) async-start(), calls=%async_computation.4 | async-start | bytes 37748736 | tf_op jit(solution)/shard_map/all_gather | solution.py:16
  87.2 7.4 all-to-all-start
  749.7 1.9 copy-start
  1082.2 0.6 copy-start.1
Sparse Core Ops, SparseCore 0:
  9.8 62.1 all-gather.3
Sparse Core Ops, SparseCore 1:
  13.2 64.7 reduce-scatter.1
  87.3 637.7 all-gather.5
